TPU v7x, 128 devices: a whole 4x4x4 slice. The times are simulated.
128 devices in a mesh: segment: 2 (over x_lo), seq: 16 (over z, y), mp: 4 (over x_hi, core).
Axes of the slice: x: 4 (x_hi: 2, x_lo: 2; x = x_hi * 2 + x_lo), y: 4, z: 4, core: 2. Of those that a mesh axis runs over, the one named last changes fastest.
Arguments:
- memory: bfloat16 [2, 4096, 4096], P(None, 'seq', 'mp')
- decoder_rows: bfloat16 [2, 1024, 4096], P(None, 'seq', 'mp')
- gains: bfloat16 [2, 4096], P('segment'), may hold values from 0.5 to 1.5
- weights: bfloat16 [2, 2, 4096, 4096], P('segment', None, None, 'mp')
- lengths: int32 [2], replicated, may hold values from 512 to 4096, as said below
Outputs:
- decoder_out: bfloat16 [2, 1024, 4096], P(None, 'seq', ('segment', 'mp'))
Inputs may be any that keep to these rules, and one draw needn't show every extreme that they name: memory positions of document b at or beyond lengths[b] are padding; some document has all 4096 positions.
All inputs are finite; a program needn't handle non-finite values.
Results may differ from a plain program's by a relative error of at most 0.015.
The roundings to bfloat16 on the way count: a program that leaves them out, or rounds other values in their place, can miss the bound.
Values may be sent and summed in bfloat16 or wider, within the bound.
A program may use at most 192 MiB of HBM per device.

v0:
```python
import jax
import jax.numpy as jnp
from jax import lax
from jax.sharding import PartitionSpec as P

DKV = 64
norm_eps = 1e-06
masked_score = -1e30


def passed_along(shard, axis, by):
    count = lax.axis_size(axis)
    pairs = [(i, i + by) for i in range(count) if 0 <= i + by < count]
    return lax.ppermute(shard, axis, pairs)


def rms_rows(rows, gain):
    wide = rows.astype(jnp.float32)
    inverse = lax.rsqrt(jnp.mean(wide * wide, axis=1, keepdims=True) + norm_eps)
    return (wide * inverse * gain.astype(jnp.float32)[None, :]).astype(jnp.bfloat16)


def fold_block(running, queries, key_block, value_block, first_pos, lengths):
    maxima, totals, summed = running
    doc_count, span = (key_block.shape[0], key_block.shape[1])
    heads_here = queries.shape[2]
    key_heads = key_block.reshape(doc_count, span, heads_here, DKV)
    value_heads = value_block.reshape(doc_count, span, heads_here, DKV)
    scores = jnp.einsum("bqhd,bkhd->bhqk", queries, key_heads, preferred_element_type=jnp.float32)
    positions = first_pos + lax.iota(jnp.int32, span)
    valid_keys = (positions[None, :] < lengths[:, None])[:, None, None, :]
    masked = jnp.where(valid_keys, scores, masked_score)
    new_max = jnp.maximum(maxima, jnp.max(masked, axis=-1))
    exp_scores = jnp.where(valid_keys, jnp.exp(masked - new_max[..., None]), 0.0)
    rescale = jnp.exp(maxima - new_max)
    totals = totals * rescale + jnp.sum(exp_scores, axis=-1)
    summed = summed * rescale[..., None] + jnp.einsum(
        "bhqk,bkhd->bhqd",
        exp_scores.astype(jnp.bfloat16),
        value_heads,
        preferred_element_type=jnp.float32,
    )
    return (new_max, totals, summed)


def on_device(memory, decoder_rows, gains, weights, lengths):
    segment_index = lax.axis_index("segment")
    decoding = segment_index == 1
    doc_count, mem_dev, part_width = memory.shape
    pos_dev = decoder_rows.shape[1]
    mem_count = doc_count * mem_dev
    row_count = doc_count * pos_dev
    mem_full, dec_full = (
        lax.all_gather(memory.reshape(mem_count, part_width), "mp", axis=1, tiled=True),
        lax.all_gather(decoder_rows.reshape(row_count, part_width), "mp", axis=1, tiled=True),
    )
    first_weight = weights[0, 0]
    second_weight = weights[0, 1]
    section_gain = gains[0]
    head_width = first_weight.shape[1]
    heads_here = head_width // DKV

    def encode(source):
        normed = rms_rows(source, section_gain)
        key_out = jnp.dot(normed, first_weight, preferred_element_type=jnp.float32).astype(
            jnp.bfloat16
        )
        value_out = jnp.dot(normed, second_weight, preferred_element_type=jnp.float32).astype(
            jnp.bfloat16
        )
        return (key_out, value_out)

    def skip_encode(source):
        empty = jnp.zeros((mem_count, head_width), jnp.bfloat16)
        return (empty, empty)

    key_local, value_local = lax.cond(decoding, skip_encode, encode, mem_full)
    query_rows = lax.cond(
        decoding,
        lambda source: jnp.dot(
            rms_rows(source, section_gain), first_weight, preferred_element_type=jnp.float32
        ).astype(jnp.bfloat16),
        lambda source: jnp.zeros((row_count, head_width), jnp.bfloat16),
        dec_full,
    )
    key_rows, value_rows = passed_along((key_local, value_local), "segment", 1)
    key_flat = key_rows.reshape(doc_count, mem_dev, head_width)
    value_flat = value_rows.reshape(doc_count, mem_dev, head_width)
    queries = query_rows.reshape(doc_count, pos_dev, heads_here, DKV)
    start_state = (
        jnp.full((doc_count, heads_here, pos_dev), masked_score, jnp.float32),
        jnp.zeros((doc_count, heads_here, pos_dev), jnp.float32),
        jnp.zeros((doc_count, heads_here, pos_dev, DKV), jnp.float32),
    )
    first_pos = jnp.int32(0)
    key_part = lax.all_gather(key_flat, "seq", axis=1, tiled=True)
    value_part = lax.all_gather(value_flat, "seq", axis=1, tiled=True)
    span = key_part.shape[1]
    width = 256

    def attend(state):
        for offset in range(0, span, width):
            state = fold_block(
                state,
                queries,
                key_part[:, offset : offset + width],
                value_part[:, offset : offset + width],
                first_pos + offset,
                lengths,
            )
        return state

    final_state = lax.cond(decoding, attend, lambda state: state, start_state)

    def finish(state):
        context = state[2] / state[1][..., None]
        return (
            jnp.transpose(context, (0, 2, 1, 3)).reshape(row_count, head_width).astype(jnp.bfloat16)
        )

    context_rows = lax.cond(
        decoding,
        finish,
        lambda state: jnp.zeros((row_count, head_width), jnp.bfloat16),
        final_state,
    )
    update_terms = lax.cond(
        decoding,
        lambda source: lax.dot_general(
            source, second_weight, (((1,), (1,)), ((), ())), preferred_element_type=jnp.float32
        ),
        lambda source: jnp.zeros((row_count, second_weight.shape[0]), jnp.float32),
        context_rows,
    )
    update = lax.psum_scatter(
        update_terms.astype(jnp.bfloat16), ("segment", "mp"), scatter_dimension=1, tiled=True
    ).astype(jnp.float32)
    out_width = update.shape[1]
    group_index = segment_index * lax.axis_size("mp") + lax.axis_index("mp")
    residual = lax.dynamic_slice_in_dim(dec_full, group_index * out_width, out_width, 1)
    decoder_out = (residual.astype(jnp.float32) + update).astype(jnp.bfloat16)
    return decoder_out.reshape(doc_count, pos_dev, out_width)


def solution(mesh):
    in_specs = (
        P(None, "seq", "mp"),
        P(None, "seq", "mp"),
        P("segment", None),
        P("segment", None, None, "mp"),
        P(),
    )
    out_specs = P(None, "seq", ("segment", "mp"))
    return jax.shard_map(
        on_device, mesh=mesh, in_specs=in_specs, out_specs=out_specs, check_vma=False
    )
```

profile of v0, /device:TPU:1, one launch (start us, length us, event | category | flops | bytes accessed | tf_op | source)
XLA Modules:
  0.0 470.3 jit_solution(12025478866281575327)
XLA Ops:
  6.5 0.0 all-gather.7.cloned.1.call-start
  6.5 0.7 all-gather.7.cloned.1.call-update
  7.3 0.0 all-gather.5.cloned.1.call-start
  7.3 0.7 all-gather.5.cloned.1.call-update
  8.0 0.0 copy-start.18
  8.0 0.0 all-gather.9.cloned.1.call-start
  8.1 11.7 %slice_bitcast_fusion = (bf16[4096,1024]{1,0:T(8,128)(2,1)}, bf16[4096,1024]{1,0:T(8,128)(2,1)}) fusion(bf16[1,2,4096,1024]{3,2,1,0:T(8,128)(2,1)} %param.18), kind=kLoop, calls=%fused_computation.292 | loop fusion | bytes 33554432 | tf_op jit(solution)/shard_map/squeeze | solution.py:58
  19.8 0.0 copy-done.18
  19.8 0.1 reduce
  19.8 31.4 %all-gather.7.cloned.1.call-done = bf16[512,4096]{1,0:T(8,128)(2,1)} async-done(((bf16[512,1024]{1,0:T(8,128)(2,1)}), bf16[512,4096]{1,0:T(8,128)(2,1)}) %all-gather.7.cloned.1.call-update) | async-done | bytes 4194320 | tf_op jit(solution)/shard_map/all_gather | solution.py:54
  51.2 17.2 %conditional.5 = (bf16[512,1024]{1,0:T(8,128)(2,1)S(1)}, bf16[512,1024]{1,0:T(8,128)(2,1)S(1)}) conditional(s32[]{:T(128)} %convert_element_type.104, (bf16[512,4096]{1,0:T(8,128)(2,1)}, bf16[4096]{0:T(1024)(128)(2,1)S(1)}, bf16[4096,1024]{1,0:T(8,128)(2,1)}, bf16[4096,1024]{1,0:T(8,128)(2,1)}) %tuple.43, () %tuple.44), branch_computations={%region_0.0_spmd, %region_2.0_spmd} | conditional | flops 8614055936 | bytes 73468000 | solution.py:77
  51.2 0.0 slice-start
  51.2 3.2 fusion
  54.4 0.0 slice-start.1
  54.4 0.0 copy-start
  54.5 9.3 %convolution_convert_fusion = bf16[512,1024]{1,0:T(8,128)(2,1)S(1)} fusion(bf16[4096,1024]{1,0:T(8,128)(2,1)} %get-tuple-element.48, bf16[512,4096]{1,0:T(8,128)(2,1)} %get-tuple-element.44, f32[4096]{0:T(1024)S(1)} %convert_element_type.71, f32[512]{0:T(512)S(1)} %add_rsqrt_fusion), kind=kOutput, calls=%fused_computation.5 | convolution fusion | flops 4303880192 | bytes 13649920 | tf_op jit(solution)/shard_map/cond/branch_0_fun/dot_general | solution.py:68
  63.8 0.0 slice-done
  63.8 0.0 slice-done.1
  63.8 0.0 copy-done
  63.8 4.6 convolution_convert_fusion.1
  68.4 1.4 collective-permute-start
  69.8 22.5 %collective-permute-done = bf16[512,1024]{1,0:T(8,128)(2,1)S(1)} collective-permute-done((bf16[512,1024]{1,0:T(8,128)(2,1)S(1)}, bf16[512,1024]{1,0:T(8,128)(2,1)S(1)}, u32[]{:S(2)}, u32[]{:S(2)}) %collective-permute-start) | collective-permute-done | bytes 1048608 | tf_op jit(solution)/shard_map/ppermute | solution.py:14
  92.3 0.0 copy-start.16
  92.3 1.0 copy-done.16
  93.3 0.0 all-gather.9.cloned.1.call-update
  93.3 0.0 all-gather.11.cloned.1.call-start
  93.4 4.2 collective-permute-start.1
  97.6 21.7 %collective-permute-done.1 = bf16[512,1024]{1,0:T(8,128)(2,1)S(1)} collective-permute-done((bf16[512,1024]{1,0:T(8,128)(2,1)S(1)}, bf16[512,1024]{1,0:T(8,128)(2,1)S(1)}, u32[]{:S(2)}, u32[]{:S(2)}) %collective-permute-start.1) | collective-permute-done | bytes 1048608 | tf_op jit(solution)/shard_map/ppermute | solution.py:14
  119.3 0.0 copy-start.17
  119.3 1.0 copy-done.17
  120.3 0.0 all-gather.11.cloned.1.call-update
  120.3 0.0 reduce-scatter.2.cloned.1.call-start
  120.4 0.0 all-gather.5.cloned.1.call-done
  120.4 0.0 copy-start.19
  120.4 0.1 conditional.6
  120.4 0.1 reshape.1084
  120.5 85.2 %all-gather.9.cloned.1.call-done = bf16[2,4096,1024]{2,1,0:T(8,128)(2,1)} async-done(((bf16[2,256,1024]{2,1,0:T(8,128)(2,1)}), bf16[2,4096,1024]{2,1,0:T(8,128)(2,1)}) %all-gather.9.cloned.1.call-update) | async-done | bytes 16777232 | tf_op jit(solution)/shard_map/all_gather | solution.py:96
  205.8 113.1 %all-gather.11.cloned.1.call-done = bf16[2,4096,1024]{2,1,0:T(8,128)(2,1)} async-done(((bf16[2,256,1024]{2,1,0:T(8,128)(2,1)}), bf16[2,4096,1024]{2,1,0:T(8,128)(2,1)}) %all-gather.11.cloned.1.call-update) | async-done | bytes 16777232 | tf_op jit(solution)/shard_map/all_gather | solution.py:97
  318.9 0.0 copy-done.19
  318.9 1.1 conditional.7
  318.9 1.1 broadcast_in_dim.245
  320.0 0.1 conditional.9
  320.0 0.1 broadcast.490
  320.1 0.0 copy-start.14
  320.1 1.0 copy-done.14
  321.1 0.0 reduce-scatter.2.cloned.1.call-update
  321.2 141.0 %reduce-scatter.2.cloned.1.call-done = bf16[128,512]{1,0:T(8,128)(2,1)} async-done(((bf16[128,4096]{1,0:T(8,128)(2,1)}), bf16[128,512]{1,0:T(8,128)(2,1)}) %reduce-scatter.2.cloned.1.call-update) | async-done | bytes 131088 | tf_op jit(solution)/shard_map/reduce_scatter | solution.py:135
  462.1 1.7 add_convert_fusion
  (6 shorter events, 0.1 us)
Async XLA Ops:
  6.5 44.7 %all-gather.7.cloned.1.call-start = ((), (), s32[]{:S(2)}) async-start(), calls=%async_computation.2 | async-start | bytes 5242880 | tf_op jit(solution)/shard_map/all_gather | solution.py:54
  7.3 113.2 %all-gather.5.cloned.1.call-start = ((), (), s32[]{:S(2)}) async-start(), calls=%async_computation.1 | async-start | bytes 1310720 | tf_op jit(solution)/shard_map/all_gather | solution.py:55
  8.0 11.8 %copy-start.18 = (bf16[1,4096]{1,0:T(2,128)(2,1)S(1)}, bf16[1,4096]{1,0:T(2,128)(2,1)}, u32[]{:S(2)}) copy-start(bf16[1,4096]{1,0:T(2,128)(2,1)} %param.17) | copy-start | bytes 24580
  8.0 197.8 %all-gather.9.cloned.1.call-start = ((), (), s32[]{:S(2)}) async-start(), calls=%async_computation.3 | async-start | bytes 17825792 | tf_op jit(solution)/shard_map/all_gather | solution.py:96
  51.2 12.6 %slice-start = ((s8[8388608]{0:T(1024)(128)(4,1)}), s8[4194304]{0:T(1024)(128)(4,1)S(1)}, s32[]{:S(2)}) async-start(s8[8388608]{0:T(1024)(128)(4,1)} %bitcast.82), calls=%async_computation.6 | async-start | bytes 8388608 | tf_op jit(solution)/shard_map/cond
  54.4 9.4 %slice-start.1 = ((s8[8388608]{0:T(1024)(128)(4,1)}), s8[4194304]{0:T(1024)(128)(4,1)S(1)}, s32[]{:S(2)}) async-start(s8[8388608]{0:T(1024)(128)(4,1)} %bitcast.82), calls=%async_computation.7 | async-start | bytes 8388608 | tf_op jit(solution)/shard_map/cond
  54.4 9.4 %copy-start = (bf16[512,4096]{1,0:T(8,128)(2,1)S(1)}, bf16[512,4096]{1,0:T(8,128)(2,1)}, u32[]{:S(2)}) copy-start(bf16[512,4096]{1,0:T(8,128)(2,1)} %get-tuple-element.44) | copy-start | bytes 12582916 | tf_op jit(solution)/shard_map/cond
  68.4 23.9 %collective-permute-start = (bf16[512,1024]{1,0:T(8,128)(2,1)S(1)}, bf16[512,1024]{1,0:T(8,128)(2,1)S(1)}, u32[]{:S(2)}, u32[]{:S(2)}) collective-permute-start(bf16[512,1024]{1,0:T(8,128)(2,1)S(1)} %get-tuple-element.62), channel_id=1, source_target_pairs={{0,64},{1,65},{2,66},{3,67},{4,68},{5,69},{6,70},{7,71},{8,72},{9,... | collective-permute-start | bytes 3145736 | tf_op jit(solution)/shard_map/ppermute | solution.py:14
  92.3 1.0 copy-start.16
  93.3 225.5 %all-gather.11.cloned.1.call-start = ((), (), s32[]{:S(2)}) async-start(), calls=%async_computation.4 | async-start | bytes 17825792 | tf_op jit(solution)/shard_map/all_gather | solution.py:97
  93.4 25.9 %collective-permute-start.1 = (bf16[512,1024]{1,0:T(8,128)(2,1)S(1)}, bf16[512,1024]{1,0:T(8,128)(2,1)S(1)}, u32[]{:S(2)}, u32[]{:S(2)}) collective-permute-start(bf16[512,1024]{1,0:T(8,128)(2,1)S(1)} %get-tuple-element.63), channel_id=1, source_target_pairs={{0,64},{1,65},{2,66},{3,67},{4,68},{5,69},{6,70},{7,71},{8,72},{9,... | collective-permute-start | bytes 3145736 | tf_op jit(solution)/shard_map/ppermute | solution.py:14
  119.3 1.0 copy-start.17
  120.3 341.8 %reduce-scatter.2.cloned.1.call-start = ((), (), s32[]{:S(2)}) async-start(), calls=%async_computation.5 | async-start | bytes 1179648 | tf_op jit(solution)/shard_map/reduce_scatter | solution.py:135
  120.4 198.4 %copy-start.19 = (s32[2]{0:T(128)S(1)}, s32[2]{0:T(128)}, u32[]{:S(2)}) copy-start(s32[2]{0:T(128)} %param.19) | copy-start | bytes 28
  320.1 1.0 copy-start.14
Sparse Core Ops, SparseCore 0:
  9.0 42.1 all-gather.6
  52.9 20.7 all-gather.4
  93.5 112.2 all-gather.8
  207.8 111.0 all-gather.10
  321.3 140.8 reduce-scatter.1
where the time goes:
time: 472 us; the launch traced here: 470 us
  waiting for transfers between devices  416 us (88%)
  local copies, waits for them, and re-layouts  16 us (3%)
  matrix products  13.9 us (3%)
  between operations  13.2 us (3%)
  starting transfers between devices  5.72 us (1%)
  other arithmetic  4.95 us (1%)
    reduce_scatter x1, waiting for transfers between devices, on_device(): lax.psum_scatter(update_terms.astype(jnp.bfloat16), ('segment', 'mp'), sc...  141 us
    all_gather x1, waiting for transfers between devices, on_device(): value_part = lax.all_gather(value_flat, 'seq', axis=1, tiled=True)  113 us
    all_gather x1, waiting for transfers between devices, on_device(): key_part = lax.all_gather(key_flat, 'seq', axis=1, tiled=True)  85.2 us
    ppermute x2, waiting for transfers between devices, passed_along(): return lax.ppermute(shard, axis, pairs)  44.2 us
    all_gather x1, waiting for transfers between devices, on_device(): lax.all_gather(memory.reshape(mem_count, part_width), 'mp', axis=1, tiled...  31.4 us
    squeeze x1, local copies, waits for them, and re-layouts, on_device(): second_weight = weights[0, 1]  11.7 us
  transfers between devices with their start and end apart: 7, of which 6 were waited for; matrix products, arithmetic and copies ran while one was open for 6% of the time, Pallas kernels for 0%

commit v1 on v0

--- a/solution.py
+++ b/solution.py
@@ -6,6 +6,27 @@
 DKV = 64
 norm_eps = 1e-06
 masked_score = -1e30
+
+
+def gather_around(x, axis, dim):
+    size, position, extent = (lax.axis_size(axis), lax.axis_index(axis), x.shape[dim])
+    right = [(i, (i + 1) % size) for i in range(size)]
+    downward = [(i, (i - 1) % size) for i in range(size)]
+    out = jnp.zeros((*x.shape[:dim], size * extent, *x.shape[dim + 1 :]), x.dtype)
+    out = lax.dynamic_update_slice_in_dim(out, x, position * extent, axis=dim)
+    from_left = from_right = x
+    middle = size // 2
+    for step in range(1, middle + 1):
+        from_left = lax.ppermute(from_left, axis, right)
+        out = lax.dynamic_update_slice_in_dim(
+            out, from_left, (position - step) % size * extent, axis=dim
+        )
+        if step < size - middle:
+            from_right = lax.ppermute(from_right, axis, downward)
+            out = lax.dynamic_update_slice_in_dim(
+                out, from_right, (position + step) % size * extent, axis=dim
+            )
+    return out
 
 
 def passed_along(shard, axis, by):
@@ -93,7 +114,7 @@
         jnp.zeros((doc_count, heads_here, pos_dev, DKV), jnp.float32),
     )
     first_pos = jnp.int32(0)
-    key_part = lax.all_gather(key_flat, "seq", axis=1, tiled=True)
+    key_part = gather_around(key_flat, "seq", 1)
     value_part = lax.all_gather(value_flat, "seq", axis=1, tiled=True)
     span = key_part.shape[1]
     width = 256

time: 472 us -> 549 us (1.16); the launches traced: 470 us -> 539 us
  local copies, waits for them, and re-layouts: 16 us -> 60.4 us
  starting transfers between devices: 5.72 us -> 41 us
  waiting for transfers between devices: 416 us -> 402 us
    ppermute x0 -> x15, waiting for transfers between devices: none -> 194 us  [the longest x8 186 us: gather_around(): from_left = lax.ppermute(from_left, axis, right)]
    all_gather x1, waiting for transfers between devices: 113 us -> 0.01 us  [on_device(): value_part = lax.all_gather(value_flat, 'seq', axis=1, tiled=True)]
    all_gather x1 -> x0, waiting for transfers between devices: 85.2 us -> none  [on_device(): key_part = lax.all_gather(key_flat, 'seq', axis=1, tiled=True)]
    ppermute x0 -> x15, starting transfers between devices: none -> 35.3 us  [the longest x7 33.5 us: gather_around(): from_right = lax.ppermute(from_right, axis, downward)]
    ppermute x0 -> x15, local copies, waits for them, and re-layouts: none -> 18.3 us  [the longest x8 11.8 us: gather_around(): from_left = lax.ppermute(from_left, axis, right)]
    dynamic_update_slice x0 -> x16, local copies, waits for them, and re-layouts: none -> 17.5 us  [the longest x8 8.75 us: gather_around(): lax.dynamic_update_slice_in_dim(out, from_left, (position - step) % size...]
    reduce_scatter x1, waiting for transfers between devices: 141 us -> 130 us  [on_device(): lax.psum_scatter(update_terms.astype(jnp.bfloat16), ('segment', 'mp'), sc...]
    broadcast_in_dim x0 -> x1, local copies, waits for them, and re-layouts: none -> 5.95 us  [gather_around(): jnp.zeros((*x.shape[:dim], size * extent, *x.shape[dim + 1:]), x.dtype)]
  transfers between devices with their start and end apart: 7 -> 21, of which waited for: 6 -> 13; matrix products, arithmetic and copies ran while one was open for 6% -> 13% of each run, Pallas kernels for 0% -> 0%
where the time goes in v1:
time: 549 us; the launch traced here: 539 us
  waiting for transfers between devices  402 us (73%)
  local copies, waits for them, and re-layouts  60.4 us (11%)
  starting transfers between devices  41 us (7%)
  between operations  14 us (3%)
  matrix products  13.9 us (3%)
    ppermute x8, waiting for transfers between devices, gather_around(): from_left = lax.ppermute(from_left, axis, right)  186 us
    reduce_scatter x1, waiting for transfers between devices, on_device(): lax.psum_scatter(update_terms.astype(jnp.bfloat16), ('segment', 'mp'), sc...  130 us
    ppermute x2, waiting for transfers between devices, passed_along(): return lax.ppermute(shard, axis, pairs)  44.5 us
    ppermute x7, starting transfers between devices, gather_around(): from_right = lax.ppermute(from_right, axis, downward)  33.5 us
    all_gather x1, waiting for transfers between devices, on_device(): lax.all_gather(memory.reshape(mem_count, part_width), 'mp', axis=1, tiled...  31.4 us
    ppermute x8, local copies, waits for them, and re-layouts, gather_around(): from_left = lax.ppermute(from_left, axis, right)  11.8 us
    squeeze x1, local copies, waits for them, and re-layouts, on_device(): second_weight = weights[0, 1]  11.6 us
  transfers between devices with their start and end apart: 21, of which 13 were waited for; matrix products, arithmetic and copies ran while one was open for 13% of the time, Pallas kernels for 0%

profile of v1, /device:TPU:1, one launch (start us, length us, event | category | flops | bytes accessed | tf_op | source)
XLA Modules:
  0.0 539.1 jit_solution(14498038130353133522)
XLA Ops:
  6.5 0.7 all-gather.6.cloned.1.call-update
  7.3 0.7 all-gather.4.cloned.1.call-update
  8.1 11.6 %slice_bitcast_fusion = (bf16[4096,1024]{1,0:T(8,128)(2,1)}, bf16[4096,1024]{1,0:T(8,128)(2,1)}) fusion(bf16[1,2,4096,1024]{3,2,1,0:T(8,128)(2,1)} %param.18), kind=kLoop, calls=%fused_computation.292 | loop fusion | bytes 33554432 | tf_op jit(solution)/shard_map/squeeze | solution.py:79
  19.8 31.4 %all-gather.6.cloned.1.call-done = bf16[512,4096]{1,0:T(8,128)(2,1)} async-done(((bf16[512,1024]{1,0:T(8,128)(2,1)}), bf16[512,4096]{1,0:T(8,128)(2,1)}) %all-gather.6.cloned.1.call-update) | async-done | bytes 4194320 | tf_op jit(solution)/shard_map/all_gather | solution.py:75
  51.2 17.2 %conditional.5 = (bf16[512,1024]{1,0:T(8,128)(2,1)S(1)}, bf16[512,1024]{1,0:T(8,128)(2,1)S(1)}) conditional(s32[]{:T(128)} %convert_element_type.104, (bf16[512,4096]{1,0:T(8,128)(2,1)}, bf16[4096]{0:T(1024)(128)(2,1)S(1)}, bf16[4096,1024]{1,0:T(8,128)(2,1)}, bf16[4096,1024]{1,0:T(8,128)(2,1)}) %tuple.43, () %tuple.44), branch_computations={%region_0.0_spmd, %region_2.0_spmd} | conditional | flops 8614055936 | bytes 73468000 | solution.py:98
  51.2 3.2 fusion
  54.5 9.3 %convolution_convert_fusion = bf16[512,1024]{1,0:T(8,128)(2,1)S(1)} fusion(bf16[4096,1024]{1,0:T(8,128)(2,1)} %get-tuple-element.48, bf16[512,4096]{1,0:T(8,128)(2,1)} %get-tuple-element.44, f32[4096]{0:T(1024)S(1)} %convert_element_type.71, f32[512]{0:T(512)S(1)} %add_rsqrt_fusion), kind=kOutput, calls=%fused_computation.5 | convolution fusion | flops 4303880192 | bytes 13649920 | tf_op jit(solution)/shard_map/cond/branch_0_fun/dot_general | solution.py:89
  63.8 4.6 convolution_convert_fusion.1
  68.4 1.4 collective-permute-start.16
  69.8 22.5 %collective-permute-done.16 = bf16[512,1024]{1,0:T(8,128)(2,1)S(1)} collective-permute-done((bf16[512,1024]{1,0:T(8,128)(2,1)S(1)}, bf16[512,1024]{1,0:T(8,128)(2,1)S(1)}, u32[]{:S(2)}, u32[]{:S(2)}) %collective-permute-start.16) | collective-permute-done | bytes 1048608 | tf_op jit(solution)/shard_map/ppermute | solution.py:35
  92.3 1.1 copy-done.14
  93.5 4.2 collective-permute-start
  97.7 22.0 %collective-permute-done = bf16[512,1024]{1,0:T(8,128)(2,1)S(1)} collective-permute-done((bf16[512,1024]{1,0:T(8,128)(2,1)}, bf16[512,1024]{1,0:T(8,128)(2,1)S(1)}, u32[]{:S(2)}, u32[]{:S(2)}) %collective-permute-start) | collective-permute-done | bytes 1048608 | tf_op jit(solution)/shard_map/ppermute | solution.py:35
  119.6 1.2 collective-permute-start.1
  120.8 3.6 collective-permute-start.2
  124.5 25.5 %collective-permute-done.1 = bf16[2,256,1024]{2,1,0:T(8,128)(2,1)S(1)} collective-permute-done((bf16[2,256,1024]{2,1,0:T(8,128)(2,1)S(1)}, bf16[2,256,1024]{2,1,0:T(8,128)(2,1)S(1)}, u32[]{:S(2)}, u32[]{:S(2)}) %collective-permute-start.1) | collective-permute-done | bytes 1048608 | tf_op jit(solution)/shard_map/ppermute | solution.py:20
  150.0 4.8 collective-permute-start.4
  154.8 36.2 %collective-permute-done.3 = bf16[2,256,1024]{2,1,0:T(8,128)(2,1)S(1)} collective-permute-done((bf16[2,256,1024]{2,1,0:T(8,128)(2,1)S(1)}, bf16[2,256,1024]{2,1,0:T(8,128)(2,1)S(1)}, u32[]{:S(2)}, u32[]{:S(2)}) %collective-permute-start.3) | collective-permute-done | bytes 1048608 | tf_op jit(solution)/shard_map/ppermute | solution.py:20
  191.0 4.4 collective-permute-done.4
  195.4 5.5 %collective-permute-start.6 = (bf16[2,256,1024]{2,1,0:T(8,128)(2,1)S(1)}, bf16[2,256,1024]{2,1,0:T(8,128)(2,1)S(1)}, u32[]{:S(2)}, u32[]{:S(2)}) collective-permute-start(bf16[2,256,1024]{2,1,0:T(8,128)(2,1)S(1)} %collective-permute-done.4), channel_id=1, source_target_pairs={{0,60},{4,0},{8,4},{12,8},{16,12},{20,16},{24,20},{28,24},{32,28},... | collective-permute-start | bytes 3145736 | tf_op jit(solution)/shard_map/ppermute | solution.py:25
  200.9 39.1 %collective-permute-done.5 = bf16[2,256,1024]{2,1,0:T(8,128)(2,1)S(1)} collective-permute-done((bf16[2,256,1024]{2,1,0:T(8,128)(2,1)S(1)}, bf16[2,256,1024]{2,1,0:T(8,128)(2,1)S(1)}, u32[]{:S(2)}, u32[]{:S(2)}) %collective-permute-start.5) | collective-permute-done | bytes 1048608 | tf_op jit(solution)/shard_map/ppermute | solution.py:20
  240.0 4.4 collective-permute-done.6
  244.4 5.5 %collective-permute-start.8 = (bf16[2,256,1024]{2,1,0:T(8,128)(2,1)S(1)}, bf16[2,256,1024]{2,1,0:T(8,128)(2,1)S(1)}, u32[]{:S(2)}, u32[]{:S(2)}) collective-permute-start(bf16[2,256,1024]{2,1,0:T(8,128)(2,1)S(1)} %collective-permute-done.6), channel_id=1, source_target_pairs={{0,60},{4,0},{8,4},{12,8},{16,12},{20,16},{24,20},{28,24},{32,28},... | collective-permute-start | bytes 3145736 | tf_op jit(solution)/shard_map/ppermute | solution.py:25
  250.0 38.7 %collective-permute-done.7 = bf16[2,256,1024]{2,1,0:T(8,128)(2,1)S(1)} collective-permute-done((bf16[2,256,1024]{2,1,0:T(8,128)(2,1)S(1)}, bf16[2,256,1024]{2,1,0:T(8,128)(2,1)S(1)}, u32[]{:S(2)}, u32[]{:S(2)}) %collective-permute-start.7) | collective-permute-done | bytes 1048608 | tf_op jit(solution)/shard_map/ppermute | solution.py:20
  289.2 4.8 collective-permute-start.10
  293.9 20.6 %collective-permute-done.9 = bf16[2,256,1024]{2,1,0:T(8,128)(2,1)S(1)} collective-permute-done((bf16[2,256,1024]{2,1,0:T(8,128)(2,1)S(1)}, bf16[2,256,1024]{2,1,0:T(8,128)(2,1)S(1)}, u32[]{:S(2)}, u32[]{:S(2)}) %collective-permute-start.9) | collective-permute-done | bytes 1048608 | tf_op jit(solution)/shard_map/ppermute | solution.py:20
  314.5 1.0 copy-done.15
  315.6 4.8 collective-permute-start.12
  320.4 19.8 %collective-permute-done.11 = bf16[2,256,1024]{2,1,0:T(8,128)(2,1)} collective-permute-done((bf16[2,256,1024]{2,1,0:T(8,128)(2,1)S(1)}, bf16[2,256,1024]{2,1,0:T(8,128)(2,1)}, u32[]{:S(2)}, u32[]{:S(2)}) %collective-permute-start.11) | collective-permute-done | bytes 1048608 | tf_op jit(solution)/shard_map/ppermute | solution.py:20
  341.2 5.9 %broadcast_in_dim.269 = bf16[2,4096,1024]{1,2,0:T(8,128)(2,1)} broadcast(bf16[]{:T(256)} %constant.169.clone.1), dimensions={} | broadcast | bytes 16777218 | tf_op jit(solution)/shard_map/broadcast_in_dim | solution.py:15
  347.2 1.1 constant_dynamic-update-slice_fusion.15
  349.3 1.5 copy.10
  350.8 1.1 constant_dynamic-update-slice_fusion.14
  351.9 1.1 constant_dynamic-update-slice_fusion.13
  354.0 1.5 copy.12
  355.5 1.1 constant_dynamic-update-slice_fusion.12
  356.6 1.1 constant_dynamic-update-slice_fusion.11
  358.7 1.5 copy.14
  360.2 4.5 collective-permute-start.14
  364.7 1.1 constant_dynamic-update-slice_fusion.10
  365.8 1.1 constant_dynamic-update-slice_fusion.9
  367.9 1.5 copy.16
  369.5 1.1 constant_dynamic-update-slice_fusion.8
  370.6 1.1 constant_dynamic-update-slice_fusion.7
  371.7 1.5 copy.19
  373.2 1.5 copy.18
  374.6 1.1 constant_dynamic-update-slice_fusion.6
  375.7 1.1 constant_dynamic-update-slice_fusion.5
  376.8 1.5 copy.21
  378.3 1.5 copy.20
  379.8 1.1 constant_dynamic-update-slice_fusion.4
  380.9 1.1 constant_dynamic-update-slice_fusion.3
  382.0 1.5 copy.22
  383.5 1.5 copy.23
  385.0 1.1 constant_dynamic-update-slice_fusion.2
  386.1 1.1 constant_dynamic-update-slice_fusion.1
  387.2 5.6 %collective-permute-done.15 = bf16[2,256,1024]{2,1,0:T(8,128)(2,1)} collective-permute-done((bf16[2,256,1024]{2,1,0:T(8,128)(2,1)}, bf16[2,256,1024]{2,1,0:T(8,128)(2,1)}, u32[]{:S(2)}, u32[]{:S(2)}) %collective-permute-start.15) | collective-permute-done | bytes 1048608 | tf_op jit(solution)/shard_map/ppermute | solution.py:20
  392.8 1.5 copy.24
  394.3 1.1 constant_dynamic-update-slice_fusion
  395.4 4.1 conditional.7
  395.4 1.1 broadcast_in_dim.247
  399.7 1.0 copy-done.13
  400.7 130.0 %reduce-scatter.2.cloned.1.call-done = bf16[128,512]{1,0:T(8,128)(2,1)} async-done(((bf16[128,4096]{1,0:T(8,128)(2,1)}), bf16[128,512]{1,0:T(8,128)(2,1)}) %reduce-scatter.2.cloned.1.call-update) | async-done | bytes 131088 | tf_op jit(solution)/shard_map/reduce_scatter | solution.py:156
  530.7 1.7 add_convert_fusion
  (76 shorter events, 6.0 us)
Async XLA Ops:
  6.5 44.7 %all-gather.6.cloned.1.call-start = ((), (), s32[]{:S(2)}) async-start(), calls=%async_computation.2 | async-start | bytes 5242880 | tf_op jit(solution)/shard_map/all_gather | solution.py:75
  7.3 333.3 %all-gather.4.cloned.1.call-start = ((), (), s32[]{:S(2)}) async-start(), calls=%async_computation.1 | async-start | bytes 1310720 | tf_op jit(solution)/shard_map/all_gather | solution.py:76
  8.0 11.7 %copy-start.28 = (bf16[1,4096]{1,0:T(2,128)(2,1)S(1)}, bf16[1,4096]{1,0:T(2,128)(2,1)}, u32[]{:S(2)}) copy-start(bf16[1,4096]{1,0:T(2,128)(2,1)} %param.17) | copy-start | bytes 24580
  8.0 387.4 %all-gather.8.cloned.1.call-start = ((), (), s32[]{:S(2)}) async-start(), calls=%async_computation.3 | async-start | bytes 17825792 | tf_op jit(solution)/shard_map/all_gather | solution.py:118
  51.2 12.6 %slice-start = ((s8[8388608]{0:T(1024)(128)(4,1)}), s8[4194304]{0:T(1024)(128)(4,1)S(1)}, s32[]{:S(2)}) async-start(s8[8388608]{0:T(1024)(128)(4,1)} %bitcast.82), calls=%async_computation.5 | async-start | bytes 8388608 | tf_op jit(solution)/shard_map/cond
  54.4 9.4 %slice-start.1 = ((s8[8388608]{0:T(1024)(128)(4,1)}), s8[4194304]{0:T(1024)(128)(4,1)S(1)}, s32[]{:S(2)}) async-start(s8[8388608]{0:T(1024)(128)(4,1)} %bitcast.82), calls=%async_computation.6 | async-start | bytes 8388608 | tf_op jit(solution)/shard_map/cond
  54.5 9.4 %copy-start = (bf16[512,4096]{1,0:T(8,128)(2,1)S(1)}, bf16[512,4096]{1,0:T(8,128)(2,1)}, u32[]{:S(2)}) copy-start(bf16[512,4096]{1,0:T(8,128)(2,1)} %get-tuple-element.44) | copy-start | bytes 12582916 | tf_op jit(solution)/shard_map/cond
  68.4 23.9 %copy-start.30 = (bf16[512,1024]{1,0:T(8,128)(2,1)}, bf16[512,1024]{1,0:T(8,128)(2,1)S(1)}, u32[]{:S(2)}) copy-start(bf16[512,1024]{1,0:T(8,128)(2,1)S(1)} %get-tuple-element.62) | copy-start | bytes 3145732
  68.4 23.9 %collective-permute-start.16 = (bf16[512,1024]{1,0:T(8,128)(2,1)S(1)}, bf16[512,1024]{1,0:T(8,128)(2,1)S(1)}, u32[]{:S(2)}, u32[]{:S(2)}) collective-permute-start(bf16[512,1024]{1,0:T(8,128)(2,1)S(1)} %get-tuple-element.63), channel_id=1, source_target_pairs={{0,64},{1,65},{2,66},{3,67},{4,68},{5,69},{6,70},{7,71},{8,72},{9,... | collective-permute-start | bytes 3145736 | tf_op jit(solution)/shard_map/ppermute | solution.py:35
  92.3 1.1 copy-start.14
  93.4 437.2 %reduce-scatter.2.cloned.1.call-start = ((), (), s32[]{:S(2)}) async-start(), calls=%async_computation.4 | async-start | bytes 1179648 | tf_op jit(solution)/shard_map/reduce_scatter | solution.py:156
  93.5 26.2 %collective-permute-start = (bf16[512,1024]{1,0:T(8,128)(2,1)}, bf16[512,1024]{1,0:T(8,128)(2,1)S(1)}, u32[]{:S(2)}, u32[]{:S(2)}) collective-permute-start(bf16[512,1024]{1,0:T(8,128)(2,1)} %copy-done.30), channel_id=1, source_target_pairs={{0,64},{1,65},{2,66},{3,67},{4,68},{5,69},{6,70},{7,71},{8,72},{9,... | collective-permute-start | bytes 3145736 | tf_op jit(solution)/shard_map/ppermute | solution.py:35
  119.6 30.3 %collective-permute-start.1 = (bf16[2,256,1024]{2,1,0:T(8,128)(2,1)S(1)}, bf16[2,256,1024]{2,1,0:T(8,128)(2,1)S(1)}, u32[]{:S(2)}, u32[]{:S(2)}) collective-permute-start(bf16[2,256,1024]{2,1,0:T(8,128)(2,1)S(1)} %bitcast.118), channel_id=1, source_target_pairs={{0,4},{4,8},{8,12},{12,16},{16,20},{20,24},{24,28},{28,32},{32,36}... | collective-permute-start | bytes 3145736 | tf_op jit(solution)/shard_map/ppermute | solution.py:20
  120.8 29.2 %collective-permute-start.2 = (bf16[2,256,1024]{2,1,0:T(8,128)(2,1)S(1)}, bf16[2,256,1024]{2,1,0:T(8,128)(2,1)S(1)}, u32[]{:S(2)}, u32[]{:S(2)}) collective-permute-start(bf16[2,256,1024]{2,1,0:T(8,128)(2,1)S(1)} %bitcast.119), channel_id=1, source_target_pairs={{0,60},{4,0},{8,4},{12,8},{16,12},{20,16},{24,20},{28,24},{32,28},... | collective-permute-start | bytes 3145736 | tf_op jit(solution)/shard_map/ppermute | solution.py:25
  150.0 50.9 %copy-start.18 = (bf16[2,256,1024]{2,1,0:T(8,128)(2,1)}, bf16[2,256,1024]{2,1,0:T(8,128)(2,1)S(1)}, u32[]{:S(2)}) copy-start(bf16[2,256,1024]{2,1,0:T(8,128)(2,1)S(1)} %collective-permute-done.1) | copy-start | bytes 3145732
  150.0 41.0 %collective-permute-start.3 = (bf16[2,256,1024]{2,1,0:T(8,128)(2,1)S(1)}, bf16[2,256,1024]{2,1,0:T(8,128)(2,1)S(1)}, u32[]{:S(2)}, u32[]{:S(2)}) collective-permute-start(bf16[2,256,1024]{2,1,0:T(8,128)(2,1)S(1)} %collective-permute-done.1), channel_id=1, source_target_pairs={{0,4},{4,8},{8,12},{12,16},{16,20},{20,24},{24,28},{28,32},{32,36}... | collective-permute-start | bytes 3145736 | tf_op jit(solution)/shard_map/ppermute | solution.py:20
  150.0 90.0 %copy-start.22 = (bf16[2,256,1024]{2,1,0:T(8,128)(2,1)}, bf16[2,256,1024]{2,1,0:T(8,128)(2,1)S(1)}, u32[]{:S(2)}) copy-start(bf16[2,256,1024]{2,1,0:T(8,128)(2,1)S(1)} %collective-permute-done.2) | copy-start | bytes 3145732
  150.0 45.4 %collective-permute-start.4 = (bf16[2,256,1024]{2,1,0:T(8,128)(2,1)S(1)}, bf16[2,256,1024]{2,1,0:T(8,128)(2,1)S(1)}, u32[]{:S(2)}, u32[]{:S(2)}) collective-permute-start(bf16[2,256,1024]{2,1,0:T(8,128)(2,1)S(1)} %collective-permute-done.2), channel_id=1, source_target_pairs={{0,60},{4,0},{8,4},{12,8},{16,12},{20,16},{24,20},{28,24},{32,28},... | collective-permute-start | bytes 3145736 | tf_op jit(solution)/shard_map/ppermute | solution.py:25
  191.0 59.0 %copy-start.17 = (bf16[2,256,1024]{2,1,0:T(8,128)(2,1)}, bf16[2,256,1024]{2,1,0:T(8,128)(2,1)S(1)}, u32[]{:S(2)}) copy-start(bf16[2,256,1024]{2,1,0:T(8,128)(2,1)S(1)} %collective-permute-done.3) | copy-start | bytes 3145732
  191.0 49.0 %collective-permute-start.5 = (bf16[2,256,1024]{2,1,0:T(8,128)(2,1)S(1)}, bf16[2,256,1024]{2,1,0:T(8,128)(2,1)S(1)}, u32[]{:S(2)}, u32[]{:S(2)}) collective-permute-start(bf16[2,256,1024]{2,1,0:T(8,128)(2,1)S(1)} %collective-permute-done.3), channel_id=1, source_target_pairs={{0,4},{4,8},{8,12},{12,16},{16,20},{20,24},{24,28},{28,32},{32,36}... | collective-permute-start | bytes 3145736 | tf_op jit(solution)/shard_map/ppermute | solution.py:20
  195.4 144.8 %copy-start.24 = (bf16[2,256,1024]{2,1,0:T(8,128)(2,1)}, bf16[2,256,1024]{2,1,0:T(8,128)(2,1)S(1)}, u32[]{:S(2)}) copy-start(bf16[2,256,1024]{2,1,0:T(8,128)(2,1)S(1)} %collective-permute-done.4) | copy-start | bytes 3145732
  195.4 49.0 %collective-permute-start.6 = (bf16[2,256,1024]{2,1,0:T(8,128)(2,1)S(1)}, bf16[2,256,1024]{2,1,0:T(8,128)(2,1)S(1)}, u32[]{:S(2)}, u32[]{:S(2)}) collective-permute-start(bf16[2,256,1024]{2,1,0:T(8,128)(2,1)S(1)} %collective-permute-done.4), channel_id=1, source_target_pairs={{0,60},{4,0},{8,4},{12,8},{16,12},{20,16},{24,20},{28,24},{32,28},... | collective-permute-start | bytes 3145736 | tf_op jit(solution)/shard_map/ppermute | solution.py:25
  240.0 100.1 %copy-start.19 = (bf16[2,256,1024]{2,1,0:T(8,128)(2,1)}, bf16[2,256,1024]{2,1,0:T(8,128)(2,1)S(1)}, u32[]{:S(2)}) copy-start(bf16[2,256,1024]{2,1,0:T(8,128)(2,1)S(1)} %collective-permute-done.5) | copy-start | bytes 3145732
  240.0 48.6 %collective-permute-start.7 = (bf16[2,256,1024]{2,1,0:T(8,128)(2,1)S(1)}, bf16[2,256,1024]{2,1,0:T(8,128)(2,1)S(1)}, u32[]{:S(2)}, u32[]{:S(2)}) collective-permute-start(bf16[2,256,1024]{2,1,0:T(8,128)(2,1)S(1)} %collective-permute-done.5), channel_id=1, source_target_pairs={{0,4},{4,8},{8,12},{12,16},{16,20},{20,24},{24,28},{28,32},{32,36}... | collective-permute-start | bytes 3145736 | tf_op jit(solution)/shard_map/ppermute | solution.py:20
  244.4 95.7 %copy-start.26 = (bf16[2,256,1024]{2,1,0:T(8,128)(2,1)}, bf16[2,256,1024]{2,1,0:T(8,128)(2,1)S(1)}, u32[]{:S(2)}) copy-start(bf16[2,256,1024]{2,1,0:T(8,128)(2,1)S(1)} %collective-permute-done.6) | copy-start | bytes 3145732
  244.4 44.7 %collective-permute-start.8 = (bf16[2,256,1024]{2,1,0:T(8,128)(2,1)S(1)}, bf16[2,256,1024]{2,1,0:T(8,128)(2,1)S(1)}, u32[]{:S(2)}, u32[]{:S(2)}) collective-permute-start(bf16[2,256,1024]{2,1,0:T(8,128)(2,1)S(1)} %collective-permute-done.6), channel_id=1, source_target_pairs={{0,60},{4,0},{8,4},{12,8},{16,12},{20,16},{24,20},{28,24},{32,28},... | collective-permute-start | bytes 3145736 | tf_op jit(solution)/shard_map/ppermute | solution.py:25
  288.7 51.5 %copy-start.16 = (bf16[2,256,1024]{2,1,0:T(8,128)(2,1)}, bf16[2,256,1024]{2,1,0:T(8,128)(2,1)S(1)}, u32[]{:S(2)}) copy-start(bf16[2,256,1024]{2,1,0:T(8,128)(2,1)S(1)} %collective-permute-done.7) | copy-start | bytes 3145732
  288.7 25.8 %collective-permute-start.9 = (bf16[2,256,1024]{2,1,0:T(8,128)(2,1)S(1)}, bf16[2,256,1024]{2,1,0:T(8,128)(2,1)S(1)}, u32[]{:S(2)}, u32[]{:S(2)}) collective-permute-start(bf16[2,256,1024]{2,1,0:T(8,128)(2,1)S(1)} %collective-permute-done.7), channel_id=1, source_target_pairs={{0,4},{4,8},{8,12},{12,16},{16,20},{20,24},{24,28},{28,32},{32,36}... | collective-permute-start | bytes 3145736 | tf_op jit(solution)/shard_map/ppermute | solution.py:20
  289.1 51.0 %copy-start.20 = (bf16[2,256,1024]{2,1,0:T(8,128)(2,1)}, bf16[2,256,1024]{2,1,0:T(8,128)(2,1)S(1)}, u32[]{:S(2)}) copy-start(bf16[2,256,1024]{2,1,0:T(8,128)(2,1)S(1)} %collective-permute-done.8) | copy-start | bytes 3145732
  289.2 26.4 %collective-permute-start.10 = (bf16[2,256,1024]{2,1,0:T(8,128)(2,1)S(1)}, bf16[2,256,1024]{2,1,0:T(8,128)(2,1)}, u32[]{:S(2)}, u32[]{:S(2)}) collective-permute-start(bf16[2,256,1024]{2,1,0:T(8,128)(2,1)S(1)} %collective-permute-done.8), channel_id=1, source_target_pairs={{0,60},{4,0},{8,4},{12,8},{16,12},{20,16},{24,20},{28,24},{32,28},... | collective-permute-start | bytes 3145736 | tf_op jit(solution)/shard_map/ppermute | solution.py:25
  314.5 1.0 copy-start.15
  315.6 24.6 %collective-permute-start.11 = (bf16[2,256,1024]{2,1,0:T(8,128)(2,1)S(1)}, bf16[2,256,1024]{2,1,0:T(8,128)(2,1)}, u32[]{:S(2)}, u32[]{:S(2)}) collective-permute-start(bf16[2,256,1024]{2,1,0:T(8,128)(2,1)S(1)} %collective-permute-done.9), channel_id=1, source_target_pairs={{0,4},{4,8},{8,12},{12,16},{16,20},{20,24},{24,28},{28,32},{32,36}... | collective-permute-start | bytes 3145736 | tf_op jit(solution)/shard_map/ppermute | solution.py:20
  315.6 44.6 %collective-permute-start.12 = (bf16[2,256,1024]{2,1,0:T(8,128)(2,1)}, bf16[2,256,1024]{2,1,0:T(8,128)(2,1)}, u32[]{:S(2)}, u32[]{:S(2)}) collective-permute-start(bf16[2,256,1024]{2,1,0:T(8,128)(2,1)} %collective-permute-done.10), channel_id=1, source_target_pairs={{0,60},{4,0},{8,4},{12,8},{16,12},{20,16},{24,20},{28,24},{32,28},... | collective-permute-start | bytes 3145736 | tf_op jit(solution)/shard_map/ppermute | solution.py:25
  340.2 29.2 %collective-permute-start.13 = (bf16[2,256,1024]{2,1,0:T(8,128)(2,1)}, bf16[2,256,1024]{2,1,0:T(8,128)(2,1)}, u32[]{:S(2)}, u32[]{:S(2)}) collective-permute-start(bf16[2,256,1024]{2,1,0:T(8,128)(2,1)} %collective-permute-done.11), channel_id=1, source_target_pairs={{0,4},{4,8},{8,12},{12,16},{16,20},{20,24},{24,28},{28,32},{32,36}... | collective-permute-start | bytes 3145736 | tf_op jit(solution)/shard_map/ppermute | solution.py:20
  347.2 1.6 copy-start.23
  351.9 1.6 copy-start.25
  356.6 1.6 copy-start.27
  360.2 23.3 %collective-permute-start.14 = (bf16[2,256,1024]{2,1,0:T(8,128)(2,1)}, bf16[2,256,1024]{2,1,0:T(8,128)(2,1)}, u32[]{:S(2)}, u32[]{:S(2)}) collective-permute-start(bf16[2,256,1024]{2,1,0:T(8,128)(2,1)} %collective-permute-done.12), channel_id=1, source_target_pairs={{0,60},{4,0},{8,4},{12,8},{16,12},{20,16},{24,20},{28,24},{32,28},... | collective-permute-start | bytes 3145736 | tf_op jit(solution)/shard_map/ppermute | solution.py:25
  365.8 1.6 copy-start.21
  369.4 23.4 %collective-permute-start.15 = (bf16[2,256,1024]{2,1,0:T(8,128)(2,1)}, bf16[2,256,1024]{2,1,0:T(8,128)(2,1)}, u32[]{:S(2)}, u32[]{:S(2)}) collective-permute-start(bf16[2,256,1024]{2,1,0:T(8,128)(2,1)} %collective-permute-done.13), channel_id=1, source_target_pairs={{0,4},{4,8},{8,12},{12,16},{16,20},{20,24},{24,28},{28,32},{32,36}... | collective-permute-start | bytes 3145736 | tf_op jit(solution)/shard_map/ppermute | solution.py:20
  387.2 8.2 %copy-start.29 = (s32[2]{0:T(128)S(1)}, s32[2]{0:T(128)}, u32[]{:S(2)}) copy-start(s32[2]{0:T(128)} %param.19) | copy-start | bytes 28
  399.7 1.0 copy-start.13
Sparse Core Ops, SparseCore 0:
  9.0 42.1 all-gather.5
  52.9 20.7 all-gather.3
  93.5 195.3 all-gather.7
  400.8 129.8 reduce-scatter.1
